TPU v7x, 128 devices: a whole 4x4x4 slice. The times are simulated.
128 devices in a mesh: row: 8 (over y, core), col: 16 (over z, x).
Axes of the slice: x: 4, y: 4, z: 4, core: 2. Of those that a mesh axis runs over, the one named last changes fastest.
Arguments:
- features: float32 [256, 1024, 128], P('row', 'col'), may hold values from -0.4 to 0.4
- step_size: float32 [256, 1024, 128], P('row', 'col'), may hold values from 0.5 to 2
- write_weights: float32 [256, 1024, 16], P('row', 'col'), may hold values from -6 to 6
- read_weights: float32 [256, 1024, 16], P('row', 'col'), may hold values from -6 to 6
- decay_log: float32 [16, 128], replicated, may hold values from -7.6 to -3.5
- out_grad: float32 [256, 1024, 128], P('row', 'col'), may hold values from -0.4 to 0.4
Outputs:
- grad_features: float32 [256, 1024, 128], P('row', 'col')
- grad_step: float32 [256, 1024, 128], P('row', 'col')
- grad_write: float32 [256, 1024, 16], P('row', 'col')
- grad_read: float32 [256, 1024, 16], P('row', 'col')
- grad_decay: float32 [16, 128], replicated
All inputs are finite; a program needn't handle non-finite values.
Results may differ from a plain program's by a relative error of at most 0.0002.
Values sent between devices are 32-bit elements; how exact they have to be, the bound alone decides.
A program may use at most 320 MiB of HBM per device.

v0:
```python
import jax
import jax.numpy as jnp
from jax import lax
from jax.sharding import PartitionSpec as P


def carried_in(shard, axis, combine, identity, reverse):
    size, mine = (lax.axis_size(axis), lax.axis_index(axis))
    everything = jax.tree.map(lambda part: lax.all_gather(part, axis), shard)
    start = jax.tree.map(
        lambda part, zero: jnp.broadcast_to(jnp.asarray(zero, part.dtype), part.shape),
        shard,
        identity,
    )

    def lap(k, before):
        at = size - 1 - k if reverse else k
        reached = at > mine if reverse else at < mine
        new = combine(before, jax.tree.map(lambda part: part[at], everything))
        return jax.tree.map(lambda a, b: jnp.where(reached, a, b), new, before)

    return lax.fori_loop(0, size, lap, start)


def sweep_rows(decays, driving, backward):

    def advance(current, inputs):
        factor, source = inputs
        current = factor * current + source
        return (current, current)

    def retreat(passed, inputs):
        factor, source = inputs
        adjoint = source + passed
        return (factor * adjoint, adjoint)

    initial = jnp.zeros(decays.shape[1:], jnp.float32)
    if backward:
        closing, values = lax.scan(retreat, initial, (decays, driving), reverse=True)
    else:
        closing, values = lax.scan(advance, initial, (decays, driving))
    return (values, closing)


def sweep_cols(decays, driving, backward):
    length = decays.shape[1]

    def advance(index, running):
        current, values = running
        place = length - 1 - index if backward else index
        place = jnp.asarray(place).astype(jnp.int32)
        factor = lax.dynamic_index_in_dim(decays, place, 1, keepdims=False)
        source = lax.dynamic_index_in_dim(driving, place, 1, keepdims=False)
        if backward:
            value = source + current
            values = lax.dynamic_update_index_in_dim(values, value, place, 1)
            current = factor * value
        else:
            current = factor * current + source
            values = lax.dynamic_update_index_in_dim(values, current, place, 1)
        return (current, values)

    initial = jnp.zeros(decays.shape[:1] + decays.shape[2:], jnp.float32)
    closing, values = lax.fori_loop(0, length, advance, (initial, jnp.zeros_like(driving)))
    return (values, closing)


def link_parts(final_state, exponent_sum, decay_rate):

    def combine(earlier, subsequent):
        return (earlier[0] * subsequent[0], subsequent[0] * earlier[1] + subsequent[1])

    products = jnp.exp(exponent_sum[:, None, :] * decay_rate)
    element = (products, final_state)
    identity = (jnp.ones_like(products), jnp.zeros_like(final_state))
    return (element, identity, combine)


def shards(features, step_size, write_weights, read_weights, decay_log, out_grad):
    highest = lax.Precision.HIGHEST
    decay_rate = -jnp.exp(decay_log)
    decays = jnp.exp(step_size[:, :, None, :] * decay_rate)
    driving = step_size[:, :, None, :] * write_weights[:, :, :, None] * features[:, :, None, :]
    running_rows = jnp.cumsum(step_size, 0)
    running_cols = jnp.cumsum(step_size, 1)
    sum_rows = running_rows[-1]
    sum_cols = running_cols[:, -1]
    local_rows, leaving_rows = sweep_rows(decays, driving, False)
    element, identity, combine = link_parts(leaving_rows, sum_rows, decay_rate)
    from_above = carried_in(element, "row", combine, identity, False)[1]
    vertical = local_rows + jnp.exp(running_rows[:, :, None, :] * decay_rate) * from_above[None]
    vert_prev = jnp.concatenate([from_above[None], vertical[:-1]], 0)
    local_cols, leaving_cols = sweep_cols(decays, vertical, False)
    element, identity, combine = link_parts(leaving_cols, sum_cols, decay_rate)
    from_left = carried_in(element, "col", combine, identity, False)[1]
    states = local_cols + jnp.exp(running_cols[:, :, None, :] * decay_rate) * from_left[:, None]
    states_prev = jnp.concatenate([from_left[:, None], states[:, :-1]], 1)
    direct = read_weights[:, :, :, None] * out_grad[:, :, None, :]
    adjoint_local, outgoing_cols = sweep_cols(decays, direct, True)
    element, identity, combine = link_parts(outgoing_cols, sum_cols, decay_rate)
    from_right = carried_in(element, "col", combine, identity, True)[1]
    after_cols = sum_cols[:, None, :] - running_cols
    adjoint_h = (
        adjoint_local + jnp.exp(after_cols[:, :, None, :] * decay_rate) * from_right[:, None]
    )
    adjoint_vlocal, outgoing_rows = sweep_rows(decays, adjoint_h, True)
    element, identity, combine = link_parts(outgoing_rows, sum_rows, decay_rate)
    from_below = carried_in(element, "row", combine, identity, True)[1]
    after_rows = sum_rows[None] - running_rows
    adjoint_v = adjoint_vlocal + jnp.exp(after_rows[:, :, None, :] * decay_rate) * from_below[None]
    exponent_grad = (adjoint_h * states_prev + adjoint_v * vert_prev) * decays
    through = jnp.einsum("hwnd,hwn->hwd", adjoint_v, write_weights, precision=highest)
    grad_features = step_size * through
    grad_step = features * through + jnp.einsum(
        "hwnd,nd->hwd", exponent_grad, decay_rate, precision=highest
    )
    grad_write = jnp.einsum("hwnd,hwd->hwn", adjoint_v, step_size * features, precision=highest)
    grad_read = jnp.einsum("hwnd,hwd->hwn", states, out_grad, precision=highest)
    partial_sum = jnp.einsum("hwnd,hwd->nd", exponent_grad, step_size, precision=highest)
    grad_decay = lax.psum(partial_sum, ("row", "col")) * decay_rate
    return (grad_features, grad_step, grad_write, grad_read, grad_decay)


def solution(mesh):
    in_specs = (
        P("row", "col", None),
        P("row", "col", None),
        P("row", "col", None),
        P("row", "col", None),
        P(),
        P("row", "col", None),
    )
    out_specs = (
        P("row", "col", None),
        P("row", "col", None),
        P("row", "col", None),
        P("row", "col", None),
        P(),
    )
    return jax.shard_map(shards, mesh=mesh, in_specs=in_specs, out_specs=out_specs, check_vma=False)
```

profile of v0, /device:TPU:1, one launch (start us, length us, event | category | flops | bytes accessed | tf_op | source)
XLA Modules:
  0.0 968.1 jit_solution(15481916507911445551)
XLA Ops:
  13.7 9.3 multiply_multiply_fusion
  35.0 7.9 broadcast.59.clone3
  42.9 79.4 %while.128 = (s32[]{:T(128)}, f32[64,16,128]{2,1,0:T(8,128)S(1)}, f32[32,64,16,128]{3,2,0,1:T(8,128)}, f32[32,64,16,128]{3,2,1,0:T(8,128)}, f32[32,64,16,128]{3,2,0,1:T(8,128)}, /*index=5*/s32[]{:T(128)}, s32[]{:T(128)}) while((s32[]{:T(128)}, f32[64,16,128]{2,1,0:T(8,128)S(1)}, f32[32,64,16,128]{3,2,0,1:T(8,128)}, ...), condition=%wide.region_11.12_spmd.clone, body=%wide.region_10.11_spmd.clone.sunk | while | flops 393219 | bytes 2622039 | solution.py:41
  141.8 8.0 broadcast.59.clone3.2
  149.7 186.2 %while.124 = (s32[]{:T(128)}, f32[32,16,128]{2,1,0:T(8,128)S(1)}, f32[32,64,16,128]{3,2,0,1:T(8,128)}, f32[32,64,16,128]{3,2,0,1:T(8,128)}, f32[32,64,16,128]{3,...) while((s32[]{:T(128)}, f32[32,16,128]{2,1,0:T(8,128)S(1)}, ...), condition=%wide.region_1.2_spmd.clone, body=%wide.region_0.0_spmd.clone.sunk | while | flops 327687 | bytes 1835166 | solution.py:64
  338.5 13.5 %while.129 = (s32[]{:T(128)}, f32[64,16,128]{2,1,0:T(8,128)S(1)}, s32[]{:T(128)}, f32[8,64,16,128]{3,2,1,0:T(8,128)}, f32[8,64,16,128]{3,2,1,0:T(8,128)}, /*index=5*/s32[]{:T(128)}, s32[]{:T(128)}) while((s32[]{:T(128)}, f32[64,16,128]{2,1,0:T(8,128)S(1)}, s32[]{:T(128)}, f32[8,64,16,128]{3,2,1,0:T(8,128)}, ...), condition=%wide.region_13.14_spmd.clone, body=%wide.region_12.13_spmd.clone.sunk | while | flops 524292 | bytes 2097253 | solution.py:22
  352.0 12.2 %multiply_add_fusion.1 = f32[32,64,16,128]{3,2,0,1:T(8,128)} fusion(f32[32,64,16,128]{3,2,0,1:T(8,128)} %get-tuple-element.823, f32[64,16,128]{2,1,0:T(8,128)S(1)} %get-tuple-element.825, f32[32,64,128]{2,0,1:T(8,128)} %copy.41, f32[16,128]{1,0:T(8,128)S(1)} %exponential_negate_fusion), kind=kLoop, calls=%fused_computation.33 | loop fusion | flops 12582912 | bytes 35135488 | tf_op jit(solution)/shard_map/add | solution.py:91
  364.2 8.0 broadcast.59.clone3.1
  372.2 124.9 %while.130 = (s32[]{:T(128)}, f32[32,16,128]{2,1,0:T(8,128)S(1)}, f32[32,64,16,128]{3,2,0,1:T(8,128)}, f32[32,64,16,128]{3,2,0,1:T(8,128)}, f32[32,64,16,128]{3,2,0,1:T(8,128)}, /*index=5*/s32[]{:T(128)}, s32[]{:T(128)}) while((s32[]{:T(128)}, f32[32,16,128]{2,1,0:T(8,128)S(1)}, f32[32,64,16,128]{3,2,0,1:T(8,128)}, ...), condition=%wide.region_15.16_spmd.clone, body=%wide.region_14.15_spmd.clone.sunk | while | flops 196611 | bytes 1311319 | solution.py:64
  500.2 29.8 %while.125 = (s32[]{:T(128)}, f32[32,16,128]{2,1,0:T(8,128)}, s32[]{:T(128)}, f32[16,32,16,128]{3,2,1,0:T(8,128)}, f32[16,32,16,128]{3,2,1,0:T(8,128)}, /*index=5*/s32[]{:T(128)}, s32[]{:T(128)}, s32[]{:T(128)}, s32[]{:T(128)}) while((s32[]{:T(128)}, f32[32,16,128]{2,1,0:T(8,128)}, s32[]{:T(128)}, f32[16,32,16,128]{3,2,1,0:T(8,128)}, ...), condition=%wide.region_4.5_spmd.clone, body=%wide.region_3.4_spmd.clone.sunk | while | flops 262152 | bytes 1048739 | solution.py:22
  530.0 22.9 %all-gather.21.cloned.1.call-done = f32[512,16,128]{2,1,0:T(8,128)} async-done(((f32[32,16,128]{2,1,0:T(8,128)}), f32[512,16,128]{2,1,0:T(8,128)}) %all-gather.21.cloned.1.call-update) | async-done | bytes 4194320 | tf_op jit(solution)/shard_map/all_gather | solution.py:9
  552.9 20.3 %while.131 = (s32[]{:T(128)}, f32[32,16,128]{2,1,0:T(8,128)S(1)}, s32[]{:T(128)}, f32[16,32,16,128]{3,2,1,0:T(8,128)}, f32[16,32,16,128]{3,2,1,0:T(8,128)}, /*index=5*/s32[]{:T(128)}, s32[]{:T(128)}) while((s32[]{:T(128)}, f32[32,16,128]{2,1,0:T(8,128)S(1)}, s32[]{:T(128)}, f32[16,32,16,128]{3,2,1,0:T(8,128)}, ...), condition=%wide.region_17.18_spmd.clone, body=%wide.region_16.17_spmd.clone.sunk | while | flops 262148 | bytes 1048677 | solution.py:22
  573.2 23.2 %multiply_add_fusion = (f32[32,64,16,128]{3,2,0,1:T(8,128)}, f32[32,64,16,128]{3,2,0,1:T(8,128)}) fusion(f32[32,64,16,128]{3,2,0,1:T(8,128)} %get-tuple-element.828, f32[32,16,128]{2,1,0:T(8,128)S(1)} %get-tuple-element.827, f32[32,64,128]{2,0,1:T(8,128)} %copy-done.5, f32[16,128]{1,0:T(8,128)S(1)} %exponential_negate_fusion, ...), kind=kLoop, calls=%fused_computation.32 | loop fusion | flops 25165824 | bytes 69738496 | tf_op jit(solution)/shard_map/add | solution.py:96
  596.4 7.9 broadcast.59.clone2
  604.3 113.4 %while.126 = (s32[]{:T(128)}, f32[64,16,128]{2,1,0:T(8,128)S(1)}, f32[32,64,16,128]{3,2,0,1:T(8,128)}, f32[32,64,16,128]{3,2,1,0:T(8,128)}, f32[32,64,16,128]{3,...) while((s32[]{:T(128)}, f32[64,16,128]{2,1,0:T(8,128)S(1)}, f32[32,64,16,128]{3,2,0,1:T(8,128)}, ...), condition=%wide.region_6.7_spmd.clone, body=%wide.region_5.6_spmd.clone.sunk | while | flops 655364 | bytes 3670132 | solution.py:39
  724.7 11.6 %slice.19 = f32[31,64,16,128]{3,2,0,1:T(8,128)} slice(f32[32,64,16,128]{3,2,0,1:T(8,128)} %get-tuple-element.1542), slice={[0:31], [0:64], [0:16], [0:128]} | slice | bytes 32505856 | tf_op jit(solution)/shard_map/slice | solution.py:92
  736.3 13.9 %slice.18 = f32[32,63,16,128]{3,2,0,1:T(8,128)} slice(f32[32,64,16,128]{3,2,0,1:T(8,128)} %get-tuple-element.1087), slice={[0:32], [0:63], [0:16], [0:128]} | slice | bytes 33030144 | tf_op jit(solution)/shard_map/slice | solution.py:97
  753.5 27.6 %fusion.6 = f32[32,64,1,16]{3,2,1,0:T(1,128)} fusion(f32[32,64,128,1]{2,3,1,0:T(1,128)S(1)} %bitcast.158, f32[32,64,16,128]{3,2,0,1:T(8,128)S(1)} %bitcast.152), kind=kOutput, calls=%fused_computation.29 | convolution fusion | flops 50331648 | bytes 17956864 | tf_op jit(solution)/shard_map/hwnd,hwd->hwn/dot_general | solution.py:118
  784.1 13.5 %while.127 = (s32[]{:T(128)}, f32[64,16,128]{2,1,0:T(8,128)S(1)}, s32[]{:T(128)}, f32[8,64,16,128]{3,2,1,0:T(8,128)}, f32[8,64,16,128]{3,2,1,0:T(8,128)}, /*index=5*/s32[]{:T(128)}, s32[]{:T(128)}, s32[]{:T(128)}, s32[]{:T(128)}) while((s32[]{:T(128)}, f32[64,16,128]{2,1,0:T(8,128)S(1)}, s32[]{:T(128)}, ...), condition=%wide.region_9.10_spmd.clone, body=%wide.region_8.9_spmd.clone.sunk | while | flops 524296 | bytes 2097315 | solution.py:22
  797.6 34.8 %multiply_reduce_fusion = (f32[128,16]{0,1:T(8,128)S(1)}, f32[32,64,16,128]{3,2,0,1:T(8,128)}, f32[32,64,16,128]{3,2,0,1:T(8,128)}) fusion(f32[128,32,64]{0,1,2:T(8,128)} %copy.74, f32[16,128]{1,0:T(8,128)S(1)} %exponential_negate_fusion, f32[32,64,128]{2,0,1:T(8,128)S(1)} %copy-done.7, f32[31,64,16,128]{3,2,0,1:T(8,128)} %slice.19, ...), kind=kLoop, calls=%fused_computation.28 | loop fusion | flops 50329600 | bytes 104349696 | tf_op jit(solution)/shard_map/hwnd,hwd->nd/dot_general | solution.py:119
  832.3 64.6 %psum.7 = f32[16,128]{1,0:T(8,128)S(1)} all-reduce(f32[16,128]{1,0:T(8,128)S(1)} %bitcast.166), channel_id=1, replica_groups=mesh['row'=8,'col'=16] {'row','col'}, use_global_device_ids=true, to_apply=%region_18.19 | all-reduce | flops 2048 | bytes 16384 | tf_op jit(solution)/shard_map/psum | solution.py:120
  897.5 18.2 %fusion.10 = f32[32,64,1,128]{3,2,1,0:T(1,128)S(1)} fusion(f32[32,64,16,1]{2,3,1,0:T(1,128)} %copy.44, f32[32,64,16,128]{3,2,0,1:T(8,128)} %get-tuple-element.1079), kind=kOutput, calls=%fused_computation.40 | convolution fusion | flops 50331648 | bytes 17956864 | tf_op jit(solution)/shard_map/hwnd,hwn->hwd/dot_general | solution.py:112
  915.7 10.9 %multiply_reduce_fusion.1 = f32[128,32,64]{0,1,2:T(8,128)} fusion(f32[32,64,16,128]{3,2,0,1:T(8,128)} %get-tuple-element.1078, f32[128,16]{0,1:T(8,128)S(1)} %get-tuple-element.1086), kind=kLoop, calls=%fused_computation.31 | loop fusion | flops 8126464 | bytes 17833984
  930.2 28.9 %fusion.8 = f32[32,64,1,16]{3,2,1,0:T(1,128)S(1)} fusion(f32[32,64,128,1]{2,3,1,0:T(1,128)S(1)} %bitcast.157, f32[32,64,16,128]{3,2,0,1:T(8,128)} %get-tuple-element.1079), kind=kOutput, calls=%fused_computation.38 | convolution fusion | flops 50331648 | bytes 17956864 | tf_op jit(solution)/shard_map/hwnd,hwd->hwn/dot_general | solution.py:117
  (418 shorter events, 640.9 us)
Async XLA Ops:
  7.2 331.3 %all-gather.19.cloned.1.call-start = ((), (), s32[]{:S(2)}) async-start(), calls=%async_computation.4 | async-start | bytes 4718592 | tf_op jit(solution)/shard_map/all_gather | solution.py:9
  9.8 13.2 %copy-start.6 = (f32[32,64,128]{2,0,1:T(8,128)}, f32[32,64,128]{2,0,1:T(8,128)S(1)}, u32[]{:S(2)}) copy-start(f32[32,64,128]{2,0,1:T(8,128)S(1)} %copy.27) | copy-start | bytes 3145732
  23.0 5.8 copy-start
  35.0 88.2 %copy-start.3 = (f32[32,64,128]{2,1,0:T(8,128)S(1)}, f32[32,64,128]{2,1,0:T(8,128)}, u32[]{:S(2)}) copy-start(f32[32,64,128]{2,1,0:T(8,128)} %param.23) | copy-start | bytes 3145732
  35.0 95.6 %copy-start.10 = (f32[32,64,16]{1,2,0:T(8,128)S(1)}, f32[32,64,16]{1,2,0:T(8,128)}, u32[]{:S(2)}) copy-start(f32[32,64,16]{1,2,0:T(8,128)} %param.25) | copy-start | bytes 393220
  122.3 0.8 copy-start.4
  123.1 215.4 %all-gather.13.cloned.1.call-start = ((), (), s32[]{:S(2)}) async-start(), calls=%async_computation.1 | async-start | bytes 4718592 | tf_op jit(solution)/shard_map/all_gather | solution.py:9
  128.1 372.1 %all-gather.11.cloned.1.call-start = ((), (), s32[]{:S(2)}) async-start(), calls=%async_computation | async-start | bytes 4456448 | tf_op jit(solution)/shard_map/all_gather | solution.py:9
  128.7 1.0 copy-start.5
  130.5 369.7 %all-gather.15.cloned.1.call-start = ((), (), s32[]{:S(2)}) async-start(), calls=%async_computation.2 | async-start | bytes 4456448 | tf_op jit(solution)/shard_map/all_gather | solution.py:9
  336.0 0.7 copy-start.2
  336.7 216.2 %all-gather.21.cloned.1.call-start = ((), (), s32[]{:S(2)}) async-start(), calls=%async_computation.5 | async-start | bytes 4456448 | tf_op jit(solution)/shard_map/all_gather | solution.py:9
  497.1 0.7 copy-start.8
  497.8 286.3 %all-gather.17.cloned.1.call-start = ((), (), s32[]{:S(2)}) async-start(), calls=%async_computation.3 | async-start | bytes 4718592 | tf_op jit(solution)/shard_map/all_gather | solution.py:9
  717.7 0.8 copy-start.1
  736.2 14.0 %slice-start = ((s8[16777216]{0:T(1024)(128)(4,1)}), s8[4194304]{0:T(1024)(128)(4,1)S(1)}, s32[]{:S(2)}) async-start(s8[16777216]{0:T(1024)(128)(4,1)} %bitcast.151), calls=%async_computation.6 | async-start | bytes 8388608
  736.2 14.0 %copy-start.9 = (f32[32,64,128]{2,1,0:T(8,128)S(1)}, f32[32,64,128]{2,1,0:T(8,128)}, u32[]{:S(2)}) copy-start(f32[32,64,128]{2,1,0:T(8,128)} %param.27) | copy-start | bytes 3145732
  736.2 14.6 %slice-start.1 = ((s8[16777216]{0:T(1024)(128)(4,1)}), s8[4194304]{0:T(1024)(128)(4,1)S(1)}, s32[]{:S(2)}) async-start(s8[16777216]{0:T(1024)(128)(4,1)} %bitcast.151), calls=%async_computation.7 | async-start | bytes 8388608
  736.3 16.1 %slice-start.2 = ((s8[16777216]{0:T(1024)(128)(4,1)}), s8[4194304]{0:T(1024)(128)(4,1)S(1)}, s32[]{:S(2)}) async-start(s8[16777216]{0:T(1024)(128)(4,1)} %bitcast.151), calls=%async_computation.8 | async-start | bytes 8388608
  736.3 17.2 %slice-start.3 = ((s8[16777216]{0:T(1024)(128)(4,1)}), s8[4194304]{0:T(1024)(128)(4,1)S(1)}, s32[]{:S(2)}) async-start(s8[16777216]{0:T(1024)(128)(4,1)} %bitcast.151), calls=%async_computation.9 | async-start | bytes 8388608
  753.5 44.0 %copy-start.7 = (f32[32,64,128]{2,0,1:T(8,128)S(1)}, f32[32,64,128]{2,0,1:T(8,128)}, u32[]{:S(2)}) copy-start(f32[32,64,128]{2,0,1:T(8,128)} %copy-done.6) | copy-start | bytes 3145732
  797.6 99.3 %copy-start.11 = (f32[16,128]{1,0:T(8,128)S(1)}, f32[16,128]{1,0:T(8,128)}, u32[]{:S(2)}) copy-start(f32[16,128]{1,0:T(8,128)} %param.26) | copy-start | bytes 24580
Sparse Core Ops, SparseCore 0:
  123.2 35.7 all-gather.18
  160.7 32.0 all-gather.12
  195.6 51.1 all-gather.10
  336.8 54.8 all-gather.14
  497.9 54.8 all-gather.20
  718.6 32.1 all-gather.16
where the time goes:
time: 984 us; the launch traced here: 968 us
  other arithmetic  690 us (70%)
  local copies, waits for them, and re-layouts  98.4 us (10%)
  matrix products  74.7 us (8%)
  blocking collectives  64.6 us (7%)
  waiting for transfers between devices  23 us (2%)
  between operations  14.6 us (1%)
    dynamic_update_slice x64, other arithmetic, sweep_rows(): closing, values = lax.scan(advance, initial, (decays, driving))  143 us
    dynamic_update_slice x64, other arithmetic, advance(): values = lax.dynamic_update_index_in_dim(values, current, place, 1)  125 us
    dynamic_update_slice x64, other arithmetic, advance(): values = lax.dynamic_update_index_in_dim(values, value, place, 1)  108 us
    mul x64, other arithmetic, advance(): current = factor * value  76.4 us
    select_n x48, other arithmetic, lap(): return jax.tree.map(lambda a, b: jnp.where(reached, a, b), new, before)  76.4 us
    psum x1, blocking collectives, shards(): grad_decay = lax.psum(partial_sum, ('row', 'col')) * decay_rate  64.6 us
    mul x32, other arithmetic, retreat(): return (factor * adjoint, adjoint)  49.2 us
    dot_general x1, other arithmetic, shards(): jnp.einsum('hwnd,hwd->nd', exponent_grad, step_size, precision=highest)  34.8 us
  transfers between devices with their start and end apart: 6, of which 1 were waited for; matrix products, arithmetic and copies ran while one was open for 48% of the time, Pallas kernels for 0%

commit v1 on v0

--- a/solution.py
+++ b/solution.py
@@ -77,6 +77,12 @@
 
 
 def shards(features, step_size, write_weights, read_weights, decay_log, out_grad):
+
+    def match_squares(vec, axis_name, mesh_name):
+        for dev in (axis_name, mesh_name):
+            vec = lax.psum(vec, dev)
+        return vec
+
     highest = lax.Precision.HIGHEST
     decay_rate = -jnp.exp(decay_log)
     decays = jnp.exp(step_size[:, :, None, :] * decay_rate)
@@ -117,7 +123,7 @@
     grad_write = jnp.einsum("hwnd,hwd->hwn", adjoint_v, step_size * features, precision=highest)
     grad_read = jnp.einsum("hwnd,hwd->hwn", states, out_grad, precision=highest)
     partial_sum = jnp.einsum("hwnd,hwd->nd", exponent_grad, step_size, precision=highest)
-    grad_decay = lax.psum(partial_sum, ("row", "col")) * decay_rate
+    grad_decay = match_squares(partial_sum, "row", "col") * decay_rate
     return (grad_features, grad_step, grad_write, grad_read, grad_decay)
 
 

time: 984 us -> 973 us (0.989)
  the two profiles are of different devices: /device:TPU:1 before, /device:TPU:0 now
where the time goes in v1:
time: 973 us; the launch traced here: 957 us
  other arithmetic  690 us (71%)
  local copies, waits for them, and re-layouts  98.5 us (10%)
  matrix products  74.7 us (8%)
  blocking collectives  53.8 us (6%)
  waiting for transfers between devices  22.3 us (2%)
  between operations  14.6 us (2%)
    dynamic_update_slice x64, other arithmetic, sweep_rows(): closing, values = lax.scan(advance, initial, (decays, driving))  143 us
    dynamic_update_slice x64, other arithmetic, advance(): values = lax.dynamic_update_index_in_dim(values, current, place, 1)  125 us
    dynamic_update_slice x64, other arithmetic, advance(): values = lax.dynamic_update_index_in_dim(values, value, place, 1)  109 us
    select_n x48, other arithmetic, lap(): return jax.tree.map(lambda a, b: jnp.where(reached, a, b), new, before)  76.3 us
    mul x64, other arithmetic, advance(): current = factor * value  76.3 us
    psum x2, blocking collectives, match_squares(): vec = lax.psum(vec, dev)  53.8 us
    mul x32, other arithmetic, retreat(): return (factor * adjoint, adjoint)  49.2 us
    dot_general x1, other arithmetic, shards(): jnp.einsum('hwnd,hwd->nd', exponent_grad, step_size, precision=highest)  34.8 us
  transfers between devices with their start and end apart: 6, of which 1 were waited for; matrix products, arithmetic and copies ran while one was open for 49% of the time, Pallas kernels for 0%

profile of v1, /device:TPU:0, one launch (start us, length us, event | category | flops | bytes accessed | tf_op | source)
XLA Modules:
  0.0 957.4 jit_solution(5432978173219175599)
XLA Ops:
  13.7 9.3 multiply_multiply_fusion
  35.0 7.9 broadcast.59.clone3
  42.9 79.4 %while.128 = (s32[]{:T(128)}, f32[64,16,128]{2,1,0:T(8,128)S(1)}, f32[32,64,16,128]{3,2,0,1:T(8,128)}, f32[32,64,16,128]{3,2,1,0:T(8,128)}, f32[32,64,16,128]{3,2,0,1:T(8,128)}, /*index=5*/s32[]{:T(128)}, s32[]{:T(128)}) while((s32[]{:T(128)}, f32[64,16,128]{2,1,0:T(8,128)S(1)}, f32[32,64,16,128]{3,2,0,1:T(8,128)}, ...), condition=%wide.region_11.12_spmd.clone, body=%wide.region_10.11_spmd.clone.sunk | while | flops 393219 | bytes 2622039 | solution.py:41
  141.8 8.0 broadcast.59.clone3.2
  149.8 186.4 %while.124 = (s32[]{:T(128)}, f32[32,16,128]{2,1,0:T(8,128)S(1)}, f32[32,64,16,128]{3,2,0,1:T(8,128)}, f32[32,64,16,128]{3,2,0,1:T(8,128)}, f32[32,64,16,128]{3,...) while((s32[]{:T(128)}, f32[32,16,128]{2,1,0:T(8,128)S(1)}, ...), condition=%wide.region_1.2_spmd.clone, body=%wide.region_0.0_spmd.clone.sunk | while | flops 327687 | bytes 1835166 | solution.py:64
  338.8 13.4 %while.129 = (s32[]{:T(128)}, f32[64,16,128]{2,1,0:T(8,128)S(1)}, s32[]{:T(128)}, f32[8,64,16,128]{3,2,1,0:T(8,128)}, f32[8,64,16,128]{3,2,1,0:T(8,128)}, /*index=5*/s32[]{:T(128)}, s32[]{:T(128)}) while((s32[]{:T(128)}, f32[64,16,128]{2,1,0:T(8,128)S(1)}, s32[]{:T(128)}, f32[8,64,16,128]{3,2,1,0:T(8,128)}, ...), condition=%wide.region_13.14_spmd.clone, body=%wide.region_12.13_spmd.clone.sunk | while | flops 524292 | bytes 2097253 | solution.py:22
  352.2 12.2 %multiply_add_fusion.1 = f32[32,64,16,128]{3,2,0,1:T(8,128)} fusion(f32[32,64,16,128]{3,2,0,1:T(8,128)} %get-tuple-element.823, f32[64,16,128]{2,1,0:T(8,128)S(1)} %get-tuple-element.825, f32[32,64,128]{2,0,1:T(8,128)} %copy.41, f32[16,128]{1,0:T(8,128)S(1)} %exponential_negate_fusion), kind=kLoop, calls=%fused_computation.33 | loop fusion | flops 12582912 | bytes 35135488 | tf_op jit(solution)/shard_map/add | solution.py:97
  364.5 8.0 broadcast.59.clone3.1
  372.4 125.2 %while.130 = (s32[]{:T(128)}, f32[32,16,128]{2,1,0:T(8,128)S(1)}, f32[32,64,16,128]{3,2,0,1:T(8,128)}, f32[32,64,16,128]{3,2,0,1:T(8,128)}, f32[32,64,16,128]{3,2,0,1:T(8,128)}, /*index=5*/s32[]{:T(128)}, s32[]{:T(128)}) while((s32[]{:T(128)}, f32[32,16,128]{2,1,0:T(8,128)S(1)}, f32[32,64,16,128]{3,2,0,1:T(8,128)}, ...), condition=%wide.region_15.16_spmd.clone, body=%wide.region_14.15_spmd.clone.sunk | while | flops 196611 | bytes 1311319 | solution.py:64
  500.8 29.8 %while.125 = (s32[]{:T(128)}, f32[32,16,128]{2,1,0:T(8,128)}, s32[]{:T(128)}, f32[16,32,16,128]{3,2,1,0:T(8,128)}, f32[16,32,16,128]{3,2,1,0:T(8,128)}, /*index=5*/s32[]{:T(128)}, s32[]{:T(128)}, s32[]{:T(128)}, s32[]{:T(128)}) while((s32[]{:T(128)}, f32[32,16,128]{2,1,0:T(8,128)}, s32[]{:T(128)}, f32[16,32,16,128]{3,2,1,0:T(8,128)}, ...), condition=%wide.region_4.5_spmd.clone, body=%wide.region_3.4_spmd.clone.sunk | while | flops 262152 | bytes 1048739 | solution.py:22
  530.5 22.2 %all-gather.21.cloned.1.call-done = f32[512,16,128]{2,1,0:T(8,128)} async-done(((f32[32,16,128]{2,1,0:T(8,128)}), f32[512,16,128]{2,1,0:T(8,128)}) %all-gather.21.cloned.1.call-update) | async-done | bytes 4194320 | tf_op jit(solution)/shard_map/all_gather | solution.py:9
  552.8 20.3 %while.131 = (s32[]{:T(128)}, f32[32,16,128]{2,1,0:T(8,128)S(1)}, s32[]{:T(128)}, f32[16,32,16,128]{3,2,1,0:T(8,128)}, f32[16,32,16,128]{3,2,1,0:T(8,128)}, /*index=5*/s32[]{:T(128)}, s32[]{:T(128)}) while((s32[]{:T(128)}, f32[32,16,128]{2,1,0:T(8,128)S(1)}, s32[]{:T(128)}, f32[16,32,16,128]{3,2,1,0:T(8,128)}, ...), condition=%wide.region_17.18_spmd.clone, body=%wide.region_16.17_spmd.clone.sunk | while | flops 262148 | bytes 1048677 | solution.py:22
  573.1 23.3 %multiply_add_fusion = (f32[32,64,16,128]{3,2,0,1:T(8,128)}, f32[32,64,16,128]{3,2,0,1:T(8,128)}) fusion(f32[32,64,16,128]{3,2,0,1:T(8,128)} %get-tuple-element.828, f32[32,16,128]{2,1,0:T(8,128)S(1)} %get-tuple-element.827, f32[32,64,128]{2,0,1:T(8,128)} %copy-done.5, f32[16,128]{1,0:T(8,128)S(1)} %exponential_negate_fusion, ...), kind=kLoop, calls=%fused_computation.32 | loop fusion | flops 25165824 | bytes 69738496 | tf_op jit(solution)/shard_map/add | solution.py:102
  604.3 113.4 %while.126 = (s32[]{:T(128)}, f32[64,16,128]{2,1,0:T(8,128)S(1)}, f32[32,64,16,128]{3,2,0,1:T(8,128)}, f32[32,64,16,128]{3,2,1,0:T(8,128)}, f32[32,64,16,128]{3,...) while((s32[]{:T(128)}, f32[64,16,128]{2,1,0:T(8,128)S(1)}, f32[32,64,16,128]{3,2,0,1:T(8,128)}, ...), condition=%wide.region_6.7_spmd.clone, body=%wide.region_5.6_spmd.clone.sunk | while | flops 655364 | bytes 3670132 | solution.py:39
  724.7 11.6 %slice.19 = f32[31,64,16,128]{3,2,0,1:T(8,128)} slice(f32[32,64,16,128]{3,2,0,1:T(8,128)} %get-tuple-element.1542), slice={[0:31], [0:64], [0:16], [0:128]} | slice | bytes 32505856 | tf_op jit(solution)/shard_map/slice | solution.py:98
  736.3 13.9 %slice.18 = f32[32,63,16,128]{3,2,0,1:T(8,128)} slice(f32[32,64,16,128]{3,2,0,1:T(8,128)} %get-tuple-element.1087), slice={[0:32], [0:63], [0:16], [0:128]} | slice | bytes 33030144 | tf_op jit(solution)/shard_map/slice | solution.py:103
  753.6 27.6 %fusion.6 = f32[32,64,1,16]{3,2,1,0:T(1,128)} fusion(f32[32,64,128,1]{2,3,1,0:T(1,128)S(1)} %bitcast.158, f32[32,64,16,128]{3,2,0,1:T(8,128)S(1)} %bitcast.152), kind=kOutput, calls=%fused_computation.29 | convolution fusion | flops 50331648 | bytes 17956864 | tf_op jit(solution)/shard_map/hwnd,hwd->hwn/dot_general | solution.py:124
  784.1 13.5 %while.127 = (s32[]{:T(128)}, f32[64,16,128]{2,1,0:T(8,128)S(1)}, s32[]{:T(128)}, f32[8,64,16,128]{3,2,1,0:T(8,128)}, f32[8,64,16,128]{3,2,1,0:T(8,128)}, /*index=5*/s32[]{:T(128)}, s32[]{:T(128)}, s32[]{:T(128)}, s32[]{:T(128)}) while((s32[]{:T(128)}, f32[64,16,128]{2,1,0:T(8,128)S(1)}, s32[]{:T(128)}, ...), condition=%wide.region_9.10_spmd.clone, body=%wide.region_8.9_spmd.clone.sunk | while | flops 524296 | bytes 2097315 | solution.py:22
  797.6 34.8 %multiply_reduce_fusion = (f32[128,16]{0,1:T(8,128)S(1)}, f32[32,64,16,128]{3,2,0,1:T(8,128)}, f32[32,64,16,128]{3,2,0,1:T(8,128)}) fusion(f32[128,32,64]{0,1,2:T(8,128)} %copy.74, f32[16,128]{1,0:T(8,128)S(1)} %exponential_negate_fusion, f32[32,64,128]{2,0,1:T(8,128)S(1)} %copy-done.7, f32[31,64,16,128]{3,2,0,1:T(8,128)} %slice.19, ...), kind=kLoop, calls=%fused_computation.28 | loop fusion | flops 50329600 | bytes 104349696 | tf_op jit(solution)/shard_map/hwnd,hwd->nd/dot_general | solution.py:125
  832.4 14.7 %psum.14 = f32[16,128]{1,0:T(8,128)S(1)} all-reduce(f32[16,128]{1,0:T(8,128)S(1)} %bitcast.166), channel_id=1, replica_groups=mesh['row'=8,'col'=16] {'row'}, use_global_device_ids=true, to_apply=%region_18.19 | all-reduce | flops 2048 | bytes 16384 | tf_op jit(solution)/shard_map/psum | solution.py:83
  847.2 39.0 %psum.15 = f32[16,128]{1,0:T(8,128)S(1)} all-reduce(f32[16,128]{1,0:T(8,128)S(1)} %psum.14), channel_id=1, replica_groups=mesh['row'=8,'col'=16] {'col'}, use_global_device_ids=true, to_apply=%region_19.20 | all-reduce | flops 2048 | bytes 16384 | tf_op jit(solution)/shard_map/psum | solution.py:83
  886.8 18.2 %fusion.10 = f32[32,64,1,128]{3,2,1,0:T(1,128)S(1)} fusion(f32[32,64,16,1]{2,3,1,0:T(1,128)} %copy.44, f32[32,64,16,128]{3,2,0,1:T(8,128)} %get-tuple-element.1079), kind=kOutput, calls=%fused_computation.40 | convolution fusion | flops 50331648 | bytes 17956864 | tf_op jit(solution)/shard_map/hwnd,hwn->hwd/dot_general | solution.py:118
  905.0 10.9 %multiply_reduce_fusion.1 = f32[128,32,64]{0,1,2:T(8,128)} fusion(f32[32,64,16,128]{3,2,0,1:T(8,128)} %get-tuple-element.1078, f32[128,16]{0,1:T(8,128)S(1)} %get-tuple-element.1086), kind=kLoop, calls=%fused_computation.31 | loop fusion | flops 8126464 | bytes 17833984
  919.6 28.9 %fusion.8 = f32[32,64,1,16]{3,2,1,0:T(1,128)S(1)} fusion(f32[32,64,128,1]{2,3,1,0:T(1,128)S(1)} %bitcast.157, f32[32,64,16,128]{3,2,0,1:T(8,128)} %get-tuple-element.1079), kind=kOutput, calls=%fused_computation.38 | convolution fusion | flops 50331648 | bytes 17956864 | tf_op jit(solution)/shard_map/hwnd,hwd->hwn/dot_general | solution.py:123
  (419 shorter events, 649.4 us)
Async XLA Ops:
  7.2 331.6 %all-gather.19.cloned.1.call-start = ((), (), s32[]{:S(2)}) async-start(), calls=%async_computation.4 | async-start | bytes 4718592 | tf_op jit(solution)/shard_map/all_gather | solution.py:9
  9.8 13.2 %copy-start.6 = (f32[32,64,128]{2,0,1:T(8,128)}, f32[32,64,128]{2,0,1:T(8,128)S(1)}, u32[]{:S(2)}) copy-start(f32[32,64,128]{2,0,1:T(8,128)S(1)} %copy.27) | copy-start | bytes 3145732
  23.0 5.8 copy-start
  35.0 88.2 %copy-start.3 = (f32[32,64,128]{2,1,0:T(8,128)S(1)}, f32[32,64,128]{2,1,0:T(8,128)}, u32[]{:S(2)}) copy-start(f32[32,64,128]{2,1,0:T(8,128)} %param.23) | copy-start | bytes 3145732
  35.0 95.6 %copy-start.10 = (f32[32,64,16]{1,2,0:T(8,128)S(1)}, f32[32,64,16]{1,2,0:T(8,128)}, u32[]{:S(2)}) copy-start(f32[32,64,16]{1,2,0:T(8,128)} %param.25) | copy-start | bytes 393220
  122.3 0.8 copy-start.4
  123.1 215.6 %all-gather.13.cloned.1.call-start = ((), (), s32[]{:S(2)}) async-start(), calls=%async_computation.1 | async-start | bytes 4718592 | tf_op jit(solution)/shard_map/all_gather | solution.py:9
  128.1 372.7 %all-gather.11.cloned.1.call-start = ((), (), s32[]{:S(2)}) async-start(), calls=%async_computation | async-start | bytes 4456448 | tf_op jit(solution)/shard_map/all_gather | solution.py:9
  128.7 1.0 copy-start.5
  130.5 370.2 %all-gather.15.cloned.1.call-start = ((), (), s32[]{:S(2)}) async-start(), calls=%async_computation.2 | async-start | bytes 4456448 | tf_op jit(solution)/shard_map/all_gather | solution.py:9
  336.2 0.7 copy-start.2
  336.9 215.8 %all-gather.21.cloned.1.call-start = ((), (), s32[]{:S(2)}) async-start(), calls=%async_computation.5 | async-start | bytes 4456448 | tf_op jit(solution)/shard_map/all_gather | solution.py:9
  497.7 0.7 copy-start.8
  498.4 285.8 %all-gather.17.cloned.1.call-start = ((), (), s32[]{:S(2)}) async-start(), calls=%async_computation.3 | async-start | bytes 4718592 | tf_op jit(solution)/shard_map/all_gather | solution.py:9
  717.7 0.8 copy-start.1
  736.3 14.0 %slice-start = ((s8[16777216]{0:T(1024)(128)(4,1)}), s8[4194304]{0:T(1024)(128)(4,1)S(1)}, s32[]{:S(2)}) async-start(s8[16777216]{0:T(1024)(128)(4,1)} %bitcast.151), calls=%async_computation.6 | async-start | bytes 8388608
  736.3 14.0 %copy-start.9 = (f32[32,64,128]{2,1,0:T(8,128)S(1)}, f32[32,64,128]{2,1,0:T(8,128)}, u32[]{:S(2)}) copy-start(f32[32,64,128]{2,1,0:T(8,128)} %param.27) | copy-start | bytes 3145732
  736.3 14.7 %slice-start.1 = ((s8[16777216]{0:T(1024)(128)(4,1)}), s8[4194304]{0:T(1024)(128)(4,1)S(1)}, s32[]{:S(2)}) async-start(s8[16777216]{0:T(1024)(128)(4,1)} %bitcast.151), calls=%async_computation.7 | async-start | bytes 8388608
  736.3 16.1 %slice-start.2 = ((s8[16777216]{0:T(1024)(128)(4,1)}), s8[4194304]{0:T(1024)(128)(4,1)S(1)}, s32[]{:S(2)}) async-start(s8[16777216]{0:T(1024)(128)(4,1)} %bitcast.151), calls=%async_computation.8 | async-start | bytes 8388608
  736.3 17.3 %slice-start.3 = ((s8[16777216]{0:T(1024)(128)(4,1)}), s8[4194304]{0:T(1024)(128)(4,1)S(1)}, s32[]{:S(2)}) async-start(s8[16777216]{0:T(1024)(128)(4,1)} %bitcast.151), calls=%async_computation.9 | async-start | bytes 8388608
  753.6 44.0 %copy-start.7 = (f32[32,64,128]{2,0,1:T(8,128)S(1)}, f32[32,64,128]{2,0,1:T(8,128)}, u32[]{:S(2)}) copy-start(f32[32,64,128]{2,0,1:T(8,128)} %copy-done.6) | copy-start | bytes 3145732
  797.6 88.6 %copy-start.11 = (f32[16,128]{1,0:T(8,128)S(1)}, f32[16,128]{1,0:T(8,128)}, u32[]{:S(2)}) copy-start(f32[16,128]{1,0:T(8,128)} %param.26) | copy-start | bytes 24580
Sparse Core Ops, SparseCore 0:
  123.2 34.5 all-gather.18
  159.6 32.0 all-gather.12
  194.4 51.5 all-gather.10
  337.1 54.1 all-gather.14
  498.5 54.2 all-gather.20
  718.6 31.6 all-gather.16
